TPU v7x, 32 devices: a whole 2x2x4 slice. The times are simulated.
32 devices in a mesh: row: 4 (over y, x), col: 8 (over z, core).
Axes of the slice: x: 2, y: 2, z: 4, core: 2. Of those that a mesh axis runs over, the one named last changes fastest.
Arguments:
- history: bfloat16 [2, 4096, 4096], P(None, 'row', 'col'), may hold values from -2 to 2, as said below
- start_strip: float32 [2, 2048, 4096], P(None, 'col', 'row'), may hold values from -6 to 6
- coupling: float32 [32], replicated, may hold values from 0.5 to 1.5
- dyson_inverse: float32 [2, 2, 64, 64], replicated, may hold values from -3 to 3, as said below
Outputs:
- earlier: float32 [2, 2048, 4096], P(None, None, 'col')
- later: float32 [2, 2048, 4096], P(None, 'col', 'row')
Inputs may be any that keep to these rules, and one draw needn't show every extreme that they name: history is anti-Hermitian: its element at row (s, a), column (t, b) is minus the complex conjugate of its element at row (t, b), column (s, a). `dyson_inverse`: each group's inverse is lower triangular in time.
All inputs are finite; a program needn't handle non-finite values.
Results may differ from a plain program's by a relative error of at most 0.0043.
Values may be sent and summed in bfloat16 or wider, within the bound.
A program may use at most 192 MiB of HBM per device.

v0:
```python
import jax
import jax.numpy as jnp
from jax import lax
from jax.sharding import PartitionSpec as P

TIME_STEP = 0.15


def complex_product(first_pair, second_pair):
    real_out = jnp.dot(first_pair[0], second_pair[0], preferred_element_type=jnp.float32) - jnp.dot(
        first_pair[1], second_pair[1], preferred_element_type=jnp.float32
    )
    imag_out = jnp.dot(first_pair[0], second_pair[1], preferred_element_type=jnp.float32) + jnp.dot(
        first_pair[1], second_pair[0], preferred_element_type=jnp.float32
    )
    return jnp.stack([real_out, imag_out])


def mirror_product(sigma_pair, tile_pair):
    contract = (((1,), (1,)), ((), ()))
    real_real = lax.dot_general(
        sigma_pair[0], tile_pair[0], contract, preferred_element_type=jnp.float32
    )
    imag_imag = lax.dot_general(
        sigma_pair[1], tile_pair[1], contract, preferred_element_type=jnp.float32
    )
    real_imag = lax.dot_general(
        sigma_pair[0], tile_pair[1], contract, preferred_element_type=jnp.float32
    )
    imag_real = lax.dot_general(
        sigma_pair[1], tile_pair[0], contract, preferred_element_type=jnp.float32
    )
    return jnp.stack([-real_real - imag_imag, real_imag - imag_real])


def self_energy(green, row_weight, col_weight):
    magnitude = green[0] * green[0] + green[1] * green[1]
    factor = -(row_weight[:, None] * col_weight[None, :]) * magnitude
    return green * factor[None]


def orbital_weights(coupling, offset, count):
    orbitals = coupling.shape[0]
    position = (offset + jnp.arange(count, dtype=jnp.int32)) % orbitals
    one_hot = (position[:, None] == jnp.arange(orbitals, dtype=jnp.int32)[None, :]).astype(
        jnp.float32
    )
    return jnp.dot(
        one_hot, coupling, precision=lax.Precision.HIGHEST, preferred_element_type=jnp.float32
    )


def dyson_apply(inverse, source):
    group_len = inverse.shape[1]
    flat_width = source.shape[1] * source.shape[2] // group_len
    flat = source.reshape(2, group_len, flat_width)
    real_out = jnp.dot(
        inverse[0], flat[0], precision=lax.Precision.HIGHEST, preferred_element_type=jnp.float32
    ) - jnp.dot(
        inverse[1], flat[1], precision=lax.Precision.HIGHEST, preferred_element_type=jnp.float32
    )
    imag_out = jnp.dot(
        inverse[0], flat[1], precision=lax.Precision.HIGHEST, preferred_element_type=jnp.float32
    ) + jnp.dot(
        inverse[1], flat[0], precision=lax.Precision.HIGHEST, preferred_element_type=jnp.float32
    )
    return jnp.stack([real_out, imag_out]).reshape(source.shape)


def shards(history, start_strip, coupling, dyson_inverse):
    col_count = lax.axis_size("col")
    row_index = lax.axis_index("row")
    col_index = lax.axis_index("col")
    strip_rows = start_strip.shape[1]
    strip_cols = start_strip.shape[2]
    group_rows = strip_rows * col_count
    tile_cols = history.shape[2]
    sigma_first = self_energy(
        start_strip,
        orbital_weights(coupling, col_index * strip_rows, strip_rows),
        orbital_weights(coupling, row_index * strip_cols, strip_cols),
    ).astype(jnp.bfloat16)
    partial_first = complex_product(lax.all_gather(sigma_first, "col", axis=1, tiled=True), history)
    shares = lax.psum_scatter(partial_first, "row", scatter_dimension=2, tiled=True)
    solved_part = dyson_apply(dyson_inverse[0], TIME_STEP * shares)
    earlier = lax.all_gather(solved_part, "row", axis=2, tiled=True)
    sigma_second = self_energy(
        earlier,
        orbital_weights(coupling, 0, group_rows),
        orbital_weights(coupling, col_index * tile_cols, tile_cols),
    ).astype(jnp.bfloat16)
    partial_second = mirror_product(sigma_second, history)
    column_shares = lax.psum_scatter(partial_second, "col", scatter_dimension=2, tiled=True)
    solved_shares = dyson_apply(dyson_inverse[1], TIME_STEP * column_shares)
    later_strip = lax.all_to_all(solved_shares, "col", split_axis=1, concat_axis=2, tiled=True)
    return (earlier, later_strip)


def solution(mesh):
    return jax.shard_map(
        shards,
        mesh=mesh,
        in_specs=(P(None, "row", "col"), P(None, "col", "row"), P(), P()),
        out_specs=(P(None, None, "col"), P(None, "col", "row")),
        check_vma=False,
    )
```

profile of v0, /device:TPU:9, one launch (start us, length us, event | category | flops | bytes accessed | tf_op | source)
XLA Modules:
  0.0 567.3 jit_solution(5969872615049134846)
XLA Ops:
  8.5 1.8 multiply_bitcast_fusion
  11.7 81.0 %all-gather.3.cloned.1.call-done = bf16[2,2048,1024]{2,1,0:T(8,128)(2,1)} async-done(((bf16[2,256,1024]{2,1,0:T(8,128)(2,1)}), bf16[2,2048,1024]{2,1,0:T(8,128)(2,1)}) %all-gather.3.cloned.1.call-update) | async-done | bytes 8388624 | tf_op jit(solution)/shard_map/all_gather | solution.py:83
  92.8 5.0 fusion.7
  97.8 2.3 fusion.8
  100.1 2.5 add_bitcast_fusion
  102.6 2.5 subtract_bitcast_fusion.2
  105.0 4.4 pad_maximum_fusion.1
  109.5 11.6 %all-gather.5.cloned.1.call-start = ((), (), s32[]{:S(2)}) async-start(), calls=%async_computation.5 | async-start | bytes 10485760 | tf_op jit(solution)/shard_map/all_gather | solution.py:86
  121.0 75.5 %reduce-scatter.3.cloned.1.call-done = f32[2,2048,128]{2,1,0:T(8,128)} async-done(((f32[2,2048,512]{2,1,0:T(8,128)}), f32[2,2048,128]{2,1,0:T(8,128)}) %reduce-scatter.3.cloned.1.call-update) | async-done | bytes 2097168 | tf_op jit(solution)/shard_map/reduce_scatter | solution.py:84
  196.5 1.8 broadcast_multiply_fusion.1
  206.5 86.4 %all-gather.5.cloned.1.call-done = f32[2,2048,512]{2,1,0:T(8,128)} async-done(((f32[2,2048,128]{2,1,0:T(8,128)}), f32[2,2048,512]{2,1,0:T(8,128)}) %all-gather.5.cloned.1.call-update) | async-done | bytes 8388624 | tf_op jit(solution)/shard_map/all_gather | solution.py:86
  292.8 5.4 fusion.6
  298.2 2.0 copy-done.2
  300.2 5.3 multiply_convert_fusion
  305.5 4.4 fusion.11
  310.0 2.4 fusion.12
  312.4 2.4 subtract_bitcast_fusion
  314.8 2.4 subtract_bitcast_fusion.1
  317.2 6.0 %pad_maximum_fusion = f32[2,2048,1024]{2,1,0:T(8,128)} fusion(f32[1,2048,1024]{2,1,0:T(8,128)S(1)} %subtract_bitcast_fusion, f32[1,2048,1024]{2,1,0:T(8,128)S(1)} %subtract_bitcast_fusion.1), kind=kLoop, calls=%fused_computation | loop fusion | flops 4194304 | bytes 33554432 | tf_op jit(solution)/shard_map/stack | solution.py:33
  323.2 167.2 %reduce-scatter.5.cloned.1.call-done = f32[2,2048,128]{2,1,0:T(8,128)} async-done(((f32[2,2048,1024]{2,1,0:T(8,128)}), f32[2,2048,128]{2,1,0:T(8,128)}) %reduce-scatter.5.cloned.1.call-update) | async-done | bytes 2097168 | tf_op jit(solution)/shard_map/reduce_scatter | solution.py:93
  490.4 1.8 broadcast_multiply_fusion
  497.4 1.9 pad_maximum_fusion.3
  499.4 50.6 %all_to_all.18 = f32[2,2048,128]{2,0,1:T(2,128)S(1)} all-to-all(f32[2,2048,128]{2,0,1:T(2,128)S(1)} %pad_maximum_fusion.3), channel_id=1, replica_groups=mesh['row'=4,'col'=8] {'col'}, dimensions={1} | all-to-all | bytes 4194304 | tf_op jit(solution)/shard_map/all_to_all | solution.py:95
  552.7 7.8 %copy.11 = f32[2,2048,512]{2,1,0:T(8,128)} copy(f32[2,2048,512]{2,1,0:T(8,128)} %all-gather.5.cloned.1.call-done) | data formatting | bytes 16777216
  (54 shorter events, 18.7 us)
Async XLA Ops:
  7.2 0.7 copy-start
  7.2 3.1 copy-start.3
  7.2 85.6 %all-gather.3.cloned.1.call-start = ((), (), s32[]{:S(2)}) async-start(), calls=%async_computation.3 | async-start | bytes 9437184 | tf_op jit(solution)/shard_map/all_gather | solution.py:83
  11.7 86.1 %copy-start.7 = (bf16[2,1024,512]{2,1,0:T(8,128)(2,1)S(1)}, bf16[2,1024,512]{2,1,0:T(8,128)(2,1)}, u32[]{:S(2)}) copy-start(bf16[2,1024,512]{2,1,0:T(8,128)(2,1)} %param.4) | copy-start | bytes 6291460
  11.7 184.8 %reduce-scatter.3.cloned.1.call-start = ((), (), s32[]{:S(2)}) async-start(), calls=%async_computation.4 | async-start | bytes 10485760 | tf_op jit(solution)/shard_map/reduce_scatter | solution.py:84
  92.8 5.0 copy-start.6
  109.5 183.4 %all-gather.5.cloned.1.call-start = ((), (), s32[]{:S(2)}) async-start(), calls=%async_computation.5 | async-start | bytes 10485760 | tf_op jit(solution)/shard_map/all_gather | solution.py:86
  198.3 0.9 copy-start.5
  205.3 285.1 %reduce-scatter.5.cloned.1.call-start = ((), (), s32[]{:S(2)}) async-start(), calls=%async_computation.6 | async-start | bytes 18874368 | tf_op jit(solution)/shard_map/reduce_scatter | solution.py:93
  292.8 7.4 %copy-start.2 = (f32[2,2048,512]{2,1,0:T(8,128)S(1)}, f32[2,2048,512]{2,1,0:T(8,128)}, u32[]{:S(2)}) copy-start(f32[2,2048,512]{2,1,0:T(8,128)} %all-gather.5.cloned.1.call-done) | copy-start | bytes 25165828
  305.5 4.5 copy-start.4
  305.5 4.5 copy-start.8
  552.7 7.8 %copy-start.1 = (f32[32]{0:T(128)S(1)}, f32[32]{0:T(128)}, u32[]{:S(2)}) copy-start(f32[32]{0:T(128)} %param.6) | copy-start | bytes 388
Sparse Core Ops, SparseCore 0:
  11.8 80.9 all-gather.2
  109.6 86.8 reduce-scatter.2
  205.5 87.3 all-gather.4
  323.3 167.0 reduce-scatter.4
where the time goes:
time: 579 us; the launch traced here: 567 us
  waiting for transfers between devices  410 us (71%)
  blocking collectives  50.6 us (9%)
  matrix products  34.2 us (6%)
  other arithmetic  31.2 us (5%)
  local copies, waits for them, and re-layouts  15.1 us (3%)
  between operations  14.5 us (3%)
  starting transfers between devices  11.7 us (2%)
    reduce_scatter x1, waiting for transfers between devices, shards(): lax.psum_scatter(partial_second, 'col', scatter_dimension=2, tiled=True)  167 us
    all_gather x1, waiting for transfers between devices, shards(): earlier = lax.all_gather(solved_part, 'row', axis=2, tiled=True)  86.4 us
    all_gather x1, waiting for transfers between devices, shards(): lax.all_gather(sigma_first, 'col', axis=1, tiled=True)  81 us
    reduce_scatter x1, waiting for transfers between devices, shards(): lax.psum_scatter(partial_first, 'row', scatter_dimension=2, tiled=True)  75.5 us
    all_to_all x1, blocking collectives, shards(): lax.all_to_all(solved_shares, 'col', split_axis=1, concat_axis=2, tiled=T...  50.6 us
  transfers between devices with their start and end apart: 4, of which 4 were waited for; matrix products, arithmetic and copies ran while one was open for 0% of the time, Pallas kernels for 0%

commit v1 on v0

--- a/solution.py
+++ b/solution.py
@@ -1,6 +1,10 @@
+import functools
+
 import jax
 import jax.numpy as jnp
 from jax import lax
+from jax.experimental import pallas as pl
+from jax.experimental.pallas import tpu as pltpu
 from jax.sharding import PartitionSpec as P
 
 TIME_STEP = 0.15
@@ -67,7 +71,344 @@
     return jnp.stack([real_out, imag_out]).reshape(source.shape)
 
 
+MESH = pl.DeviceIdType.MESH
+NN = (((1,), (0,)), ((), ()))
+NT = (((1,), (1,)), ((), ()))
+
+
+def mm(x, y, dims):
+    return lax.dot_general(x, y, dims, preferred_element_type=jnp.float32)
+
+
+def remote(src, dst, send_sem, recv_sem, row, col):
+    return pltpu.make_async_remote_copy(
+        src_ref=src,
+        dst_ref=dst,
+        send_sem=send_sem,
+        recv_sem=recv_sem,
+        device_id=(row, col),
+        device_id_type=MESH,
+    )
+
+
+def entry_barrier(row, q, core, lines, rows):
+    barrier = pltpu.get_barrier_semaphore()
+
+    def greet(to_row, to_col):
+        pl.semaphore_signal(barrier, inc=1, device_id=(to_row, to_col), device_id_type=MESH)
+
+    greet(row, 2 * q + 1 - core)
+    for k in range(1, rows):
+        greet(lax.rem(row + k, rows), 2 * q + core)
+
+    @pl.when(q > 0)
+    def _():
+        greet(row, 2 * (q - 1) + core)
+
+    @pl.when(q < lines - 1)
+    def _():
+        greet(row, 2 * (q + 1) + core)
+
+    ends = jnp.minimum(q, 1) + jnp.minimum(lines - 1 - q, 1)
+    pl.semaphore_wait(barrier, rows + ends)
+
+
+def first_kernel(lines, rows, sig, hist, out, blocks, parts, recv, local, hop_s, hop_r, pair_s, pair_r, sum_s, sum_r):
+    row = lax.axis_index("row")
+    col = lax.axis_index("col")
+    q, core = lax.div(col, 2), lax.rem(col, 2)
+    strip = sig.shape[1]
+    share = out.shape[2]
+    entry_barrier(row, q, core, lines, rows)
+
+    own = pltpu.make_async_copy(sig, blocks.at[col], local)
+    own.start()
+    own.wait()
+
+    def hop(way, s):
+        step = 1 - 2 * way
+        block = blocks.at[2 * (q - step * s) + core]
+        return remote(block, block, hop_s.at[way, s], hop_r.at[way, s], row, 2 * (q + step) + core)
+
+    def sends(way, s):
+        if way == 0:
+            return jnp.logical_and(q < lines - 1, q - s >= 0)
+        return jnp.logical_and(q > 0, q + s <= lines - 1)
+
+    def arrived(way, s):
+        if way == 0:
+            return q - 1 - s >= 0
+        return q + 1 + s <= lines - 1
+
+    def origin(way, s):
+        step = 1 - 2 * way
+        return q - step * (s + 1)
+
+    def pair(line, at):
+        block = blocks.at[2 * line + core]
+        return remote(block, block, pair_s.at[at], pair_r.at[at], row, 2 * q + 1 - core)
+
+    def spread(j, k):
+        to = lax.rem(row + k, rows)
+        return remote(
+            parts.at[j, to], recv.at[j, k - 1], sum_s.at[j, k - 1], sum_r.at[j, k - 1], to, col
+        )
+
+    def compute(j):
+        real = mm(blocks[j, 0], hist[0], NN) - mm(blocks[j, 1], hist[1], NN)
+        imag = mm(blocks[j, 0], hist[1], NN) + mm(blocks[j, 1], hist[0], NN)
+        at = pl.ds(pl.multiple_of(j * strip, strip), strip)
+        for r in range(rows):
+            cut = slice(r * share, (r + 1) * share)
+            parts[j, r, 0] = real[:, cut].astype(jnp.bfloat16)
+            parts[j, r, 1] = imag[:, cut].astype(jnp.bfloat16)
+
+            @pl.when(row == r)
+            def _():
+                out[0, at, :] = real[:, cut]
+                out[1, at, :] = imag[:, cut]
+
+        for k in range(1, rows):
+            spread(j, k).start()
+
+    for way in (0, 1):
+
+        @pl.when(sends(way, 0))
+        def _():
+            hop(way, 0).start()
+
+    pair(q, 2 * (lines - 1)).start()
+
+    def own_step(i, c):
+        @pl.when(i == 1)
+        def _():
+            pair(q, 2 * (lines - 1)).wait_recv()
+
+        compute(2 * q + core + i - 2 * core * i)
+        return c
+
+    lax.fori_loop(0, 2, own_step, 0)
+
+    def step(s, c):
+        for way in (0, 1):
+
+            @pl.when(arrived(way, s))
+            def _():
+                hop(way, s).wait_recv()
+                pair(origin(way, s), 2 * s + way).start()
+
+            @pl.when(jnp.logical_and(s < lines - 2, sends(way, s + 1)))
+            def _():
+                hop(way, s + 1).start()
+
+        def each(i, c2):
+            way, other = lax.rem(i, 2), lax.div(i, 2)
+            line = q - (1 - 2 * way) * (s + 1)
+
+            @pl.when(jnp.logical_and(line >= 0, line <= lines - 1))
+            def _():
+                @pl.when(other == 1)
+                def _():
+                    pair(line, 2 * s + way).wait_recv()
+
+                compute(2 * line + core + other - 2 * core * other)
+
+            return c2
+
+        lax.fori_loop(0, 4, each, 0)
+        return c
+
+    lax.fori_loop(0, lines - 1, step, 0)
+
+    def finish(j, c):
+        at = pl.ds(pl.multiple_of(j * strip, strip), strip)
+        for k in range(1, rows):
+            spread(j, k).wait_recv()
+        for p in (0, 1):
+            total = out[p, at, :]
+            for k in range(1, rows):
+                total += recv[j, k - 1, p].astype(jnp.float32)
+            out[p, at, :] = total
+        for k in range(1, rows):
+            spread(j, k).wait_send()
+        return c
+
+    lax.fori_loop(0, 2 * lines, finish, 0)
+    pair(q, 2 * (lines - 1)).wait_send()
+
+    def drain(s, c):
+        for way in (0, 1):
+
+            @pl.when(sends(way, s))
+            def _():
+                hop(way, s).wait_send()
+
+            @pl.when(arrived(way, s))
+            def _():
+                pair(origin(way, s), 2 * s + way).wait_send()
+
+        return c
+
+    lax.fori_loop(0, lines - 1, drain, 0)
+
+
+def second_kernel(lines, tau, hist, out, give, take, stage, land, pair_s, pair_r, hop_s, hop_r):
+    row = lax.axis_index("row")
+    col = lax.axis_index("col")
+    q, core = lax.div(col, 2), lax.rem(col, 2)
+    strip = out.shape[1]
+    entry_barrier(row, q, core, lines, 1)
+
+    def product(j):
+        at = pl.ds(pl.multiple_of(j * strip, strip), strip)
+        real_in, imag_in = tau[0, at, :], tau[1, at, :]
+        real = -mm(real_in, hist[0], NT) - mm(imag_in, hist[1], NT)
+        imag = mm(real_in, hist[1], NT) - mm(imag_in, hist[0], NT)
+        return real, imag
+
+    def pair(d):
+        return remote(
+            give.at[d], take.at[d], pair_s.at[d], pair_r.at[d], row, 2 * q + 1 - core
+        )
+
+    def hop(way, d):
+        to = q + 1 - 2 * way
+        return remote(
+            stage.at[d], land.at[way, d], hop_s.at[d], hop_r.at[way, d], row, 2 * to + core
+        )
+
+    def offer(d):
+        real, imag = product(2 * d + 1 - core)
+        give[d, 0] = real.astype(jnp.bfloat16)
+        give[d, 1] = imag.astype(jnp.bfloat16)
+        pair(d).start()
+
+    def gather(d):
+        real, imag = product(2 * d + core)
+        out[0] = real
+        out[1] = imag
+        pair(d).wait_recv()
+        for p in (0, 1):
+            out[p] += take[d, p].astype(jnp.float32)
+
+    def add(way, d):
+        hop(way, d).wait_recv()
+        for p in (0, 1):
+            out[p] += land[way, d, p].astype(jnp.float32)
+
+    def step(i, c):
+        t, way = lax.div(i, 2), lax.rem(i, 2)
+        d = (lines - 1 - t) * (1 - way) + t * way
+        far = (d - q) * (1 - 2 * way)
+
+        @pl.when(far > 0)
+        def _():
+            offer(d)
+            gather(d)
+
+            @pl.when(jnp.logical_and(way == 0, q > 0))
+            def _():
+                add(0, d)
+
+            @pl.when(jnp.logical_and(way == 1, q < lines - 1))
+            def _():
+                add(1, d)
+
+            for p in (0, 1):
+                stage[d, p] = out[p].astype(jnp.bfloat16)
+            hop(way, d).start()
+
+        return c
+
+    lax.fori_loop(0, 2 * (lines - 1), step, 0)
+    offer(q)
+    gather(q)
+
+    @pl.when(q > 0)
+    def _():
+        add(0, q)
+
+    @pl.when(q < lines - 1)
+    def _():
+        add(1, q)
+
+    def drain(d, c):
+        pair(d).wait_send()
+
+        @pl.when(d > q)
+        def _():
+            hop(0, d).wait_send()
+
+        @pl.when(d < q)
+        def _():
+            hop(1, d).wait_send()
+
+        return c
+
+    lax.fori_loop(0, lines, drain, 0)
+
+
+VMEM = pl.BlockSpec(memory_space=pltpu.VMEM)
+DMA = pltpu.SemaphoreType.DMA
+
+
+def first_sums(sigma, history, lines, rows):
+    strip, depth = sigma.shape[1:]
+    cols = 2 * lines
+    share = history.shape[2] // rows
+    bf16 = jnp.bfloat16
+    return pl.pallas_call(
+        functools.partial(first_kernel, lines, rows),
+        out_shape=jax.ShapeDtypeStruct((2, strip * cols, share), jnp.float32),
+        in_specs=[VMEM] * 2,
+        out_specs=VMEM,
+        scratch_shapes=[
+            pltpu.VMEM((cols, 2, strip, depth), bf16),
+            pltpu.VMEM((cols, rows, 2, strip, share), bf16),
+            pltpu.VMEM((cols, rows - 1, 2, strip, share), bf16),
+            DMA,
+            DMA((2, lines - 1)),
+            DMA((2, lines - 1)),
+            DMA((2 * lines - 1,)),
+            DMA((2 * lines - 1,)),
+            DMA((cols, rows - 1)),
+            DMA((cols, rows - 1)),
+        ],
+        compiler_params=pltpu.CompilerParams(
+            collective_id=0, has_side_effects=True, vmem_limit_bytes=40 * 1024 * 1024
+        ),
+        name="first_sums",
+    )(sigma, history)
+
+
+def second_sums(tau, history, lines):
+    depth = history.shape[1]
+    strip = tau.shape[1] // (2 * lines)
+    bf16 = jnp.bfloat16
+    return pl.pallas_call(
+        functools.partial(second_kernel, lines),
+        out_shape=jax.ShapeDtypeStruct((2, strip, depth), jnp.float32),
+        in_specs=[VMEM] * 2,
+        out_specs=VMEM,
+        scratch_shapes=[
+            pltpu.VMEM((lines, 2, strip, depth), bf16),
+            pltpu.VMEM((lines, 2, strip, depth), bf16),
+            pltpu.VMEM((lines, 2, strip, depth), bf16),
+            pltpu.VMEM((2, lines, 2, strip, depth), bf16),
+            DMA((lines,)),
+            DMA((lines,)),
+            DMA((lines,)),
+            DMA((2, lines)),
+        ],
+        compiler_params=pltpu.CompilerParams(
+            collective_id=1, has_side_effects=True, vmem_limit_bytes=50 * 1024 * 1024
+        ),
+        name="second_sums",
+    )(tau, history)
+
+
 def shards(history, start_strip, coupling, dyson_inverse):
+    row_count = lax.axis_size("row")
     col_count = lax.axis_size("col")
     row_index = lax.axis_index("row")
     col_index = lax.axis_index("col")
@@ -80,8 +421,13 @@
         orbital_weights(coupling, col_index * strip_rows, strip_rows),
         orbital_weights(coupling, row_index * strip_cols, strip_cols),
     ).astype(jnp.bfloat16)
-    partial_first = complex_product(lax.all_gather(sigma_first, "col", axis=1, tiled=True), history)
-    shares = lax.psum_scatter(partial_first, "row", scatter_dimension=2, tiled=True)
+    if tile_cols // row_count % 128 == 0:
+        shares = first_sums(sigma_first, history, col_count // 2, row_count)
+    else:
+        partial_first = complex_product(
+            lax.all_gather(sigma_first, "col", axis=1, tiled=True), history
+        )
+        shares = lax.psum_scatter(partial_first, "row", scatter_dimension=2, tiled=True)
     solved_part = dyson_apply(dyson_inverse[0], TIME_STEP * shares)
     earlier = lax.all_gather(solved_part, "row", axis=2, tiled=True)
     sigma_second = self_energy(
@@ -89,10 +435,10 @@
         orbital_weights(coupling, 0, group_rows),
         orbital_weights(coupling, col_index * tile_cols, tile_cols),
     ).astype(jnp.bfloat16)
-    partial_second = mirror_product(sigma_second, history)
-    column_shares = lax.psum_scatter(partial_second, "col", scatter_dimension=2, tiled=True)
-    solved_shares = dyson_apply(dyson_inverse[1], TIME_STEP * column_shares)
-    later_strip = lax.all_to_all(solved_shares, "col", split_axis=1, concat_axis=2, tiled=True)
+    solved_sigma = dyson_apply(
+        dyson_inverse[1], TIME_STEP * sigma_second.astype(jnp.float32)
+    ).astype(jnp.bfloat16)
+    later_strip = second_sums(solved_sigma, history, col_count // 2)
     return (earlier, later_strip)
 
 

time: 579 us -> 382 us (0.66); the launches traced: 567 us -> 381 us
  waiting for transfers between devices: 410 us -> 101 us
  Pallas kernels: 0 us -> 185 us
  blocking collectives: 50.6 us -> 0 us
  local copies, waits for them, and re-layouts: 15.1 us -> 32.6 us
  starting transfers between devices: 11.7 us -> 0.04 us
  other arithmetic: 31.2 us -> 22.4 us
  matrix products: 34.2 us -> 25.6 us
    reduce_scatter x2 -> x0, waiting for transfers between devices: 243 us -> none  [the longest x1 167 us: shards(): lax.psum_scatter(partial_second, 'col', scatter_dimension=2, tiled=True)]
    pallas_call x0 -> x2, Pallas kernels: none -> 185 us  [the longest x1 114 us: second_sums(): pl.pallas_call(functools.partial(second_kernel, lines), out_shape=jax.Sha...]
    all_gather x1 -> x0, waiting for transfers between devices: 81 us -> none  [shards(): lax.all_gather(sigma_first, 'col', axis=1, tiled=True)]
    all_to_all x1 -> x0, blocking collectives: 50.6 us -> none  [shards(): lax.all_to_all(solved_shares, 'col', split_axis=1, concat_axis=2, tiled=T...]
    dot_general x8 -> x0, matrix products: 23.8 us -> none  [the longest x1 4.98 us: complex_product(): jnp.dot(first_pair[0], second_pair[1], preferred_element_type=jnp.float32)]
    all_gather x1, waiting for transfers between devices: 86.4 us -> 101 us  [shards(): earlier = lax.all_gather(solved_part, 'row', axis=2, tiled=True)]
    all_gather x1, starting transfers between devices: 11.6 us -> 0.04 us  [shards(): earlier = lax.all_gather(solved_part, 'row', axis=2, tiled=True)]
    another operation x2 -> x0, other arithmetic: 10.4 us -> none  [the longest x1 6.04 us: mirror_product(): return jnp.stack([-real_real - imag_imag, real_imag - imag_real])]
  transfers between devices with their start and end apart: 4 -> 1, of which waited for: 4 -> 1; matrix products, arithmetic and copies ran while one was open for 0% -> 0% of each run, Pallas kernels for 0% -> 0%
where the time goes in v1:
time: 382 us; the launch traced here: 381 us
  Pallas kernels  185 us (48%)
  waiting for transfers between devices  101 us (26%)
  local copies, waits for them, and re-layouts  32.6 us (9%)
  matrix products  25.6 us (7%)
  other arithmetic  22.4 us (6%)
  between operations  14.3 us (4%)
    pallas_call x1, Pallas kernels, second_sums(): pl.pallas_call(functools.partial(second_kernel, lines), out_shape=jax.Sha...  114 us
    all_gather x1, waiting for transfers between devices, shards(): earlier = lax.all_gather(solved_part, 'row', axis=2, tiled=True)  101 us
    pallas_call x1, Pallas kernels, first_sums(): pl.pallas_call(functools.partial(first_kernel, lines, rows), out_shape=ja...  70.8 us
    slice x2, local copies, waits for them, and re-layouts, dyson_apply(): flat[0]  7.82 us
    unnamed x20, local copies, waits for them, and re-layouts  7.65 us
  transfers between devices with their start and end apart: 1, of which 1 were waited for; matrix products, arithmetic and copies ran while one was open for 0% of the time, Pallas kernels for 0%

profile of v1, /device:TPU:9, one launch (start us, length us, event | category | flops | bytes accessed | tf_op | source)
XLA Modules:
  0.0 380.6 jit_solution(8609270862461673298)
XLA Ops:
  8.5 1.8 multiply_bitcast_fusion
  10.3 2.0 multiply_convert_fusion.1.sig
  12.3 70.8 %first_sums.1 = f32[2,2048,128]{2,1,0:T(8,128)S(1)} custom-call(bf16[2,256,1024]{2,1,0:T(8,128)(2,1)S(1)} %multiply_convert_fusion.1.sig, bf16[2,1024,512]{2,1,0:T(8,128)(2,1)S(1)} %copy-done.2), custom_call_target="tpu_custom_call" | custom-call | tf_op jit(solution)/shard_map/first_sums/pallas_call | solution.py:360
  85.3 1.1 fusion.27
  86.4 1.1 fusion.5
  87.5 1.1 fusion.4
  88.9 1.5 pad_maximum_fusion.1
  91.5 100.9 %all-gather.2.cloned.1.call-done = f32[2,2048,512]{2,1,0:T(8,128)} async-done(((f32[2,2048,128]{2,1,0:T(8,128)}), f32[2,2048,512]{2,1,0:T(8,128)}) %all-gather.2.cloned.1.call-update) | async-done | bytes 8388624 | tf_op jit(solution)/shard_map/all_gather | solution.py:432
  192.4 5.4 %fusion.8 = f32[2048,512]{1,0:T(8,128)} fusion(f32[2,2048,512]{2,1,0:T(8,128)} %all-gather.2.cloned.1.call-done, f32[512]{0:T(512)S(1)} %bitcast.60, f32[2048]{0:T(1024)S(1)} %bitcast.58), kind=kLoop, calls=%fused_computation.15 | loop fusion | flops 6291456 | bytes 12593152 | tf_op jit(solution)/shard_map/mul | solution.py:43
  197.8 2.0 copy-done.3
  199.7 6.8 %convert_multiply_fusion = f32[2,2048,512]{2,1,0:T(8,128)} fusion(f32[2,2048,512]{2,1,0:T(8,128)S(1)} %copy-done.3, f32[2048,512]{1,0:T(8,128)} %fusion.8), kind=kLoop, calls=%fused_computation.6 | loop fusion | flops 8388608 | bytes 20971520 | tf_op jit(solution)/shard_map/mul | solution.py:439
  206.5 7.7 %fusion.50 = (f32[1,2048,512]{2,1,0:T(8,128)}, f32[1,2048,512]{2,1,0:T(8,128)}) fusion(f32[2,2048,512]{2,1,0:T(8,128)} %convert_multiply_fusion), kind=kLoop, calls=%fused_computation.78 | loop fusion | bytes 16777216 | tf_op jit(solution)/shard_map/slice | solution.py:62
  214.2 5.0 %squeeze.20 = f32[64,16384]{1,0:T(8,128)} reshape(f32[1,2048,512]{2,1,0:T(8,128)} %get-tuple-element.2) | data formatting | bytes 8388608 | tf_op jit(solution)/shard_map/squeeze | solution.py:62
  219.2 4.9 %squeeze.22 = f32[64,16384]{1,0:T(8,128)} reshape(f32[1,2048,512]{2,1,0:T(8,128)} %get-tuple-element.3) | data formatting | bytes 8388608 | tf_op jit(solution)/shard_map/squeeze | solution.py:64
  224.1 5.8 %fusion.19 = f32[16384,64]{0,1:T(8,128)S(1)} fusion(f32[64,16384]{1,0:T(8,128)} %squeeze.22, f32[2,2,64,64]{3,2,1,0:T(8,128)S(1)} %copy-done.6), kind=kOutput, calls=%fused_computation.36 | convolution fusion | flops 805306368 | bytes 8421376 | tf_op jit(solution)/shard_map/dot_general | solution.py:66
  229.9 4.2 %fusion.21 = f32[16384,64]{0,1:T(8,128)S(1)} fusion(f32[64,16384]{1,0:T(8,128)S(1)} %copy-done.4, f32[2,2,64,64]{3,2,1,0:T(8,128)S(1)} %copy-done.6), kind=kOutput, calls=%fused_computation.38 | convolution fusion | flops 805306368 | bytes 8421376 | tf_op jit(solution)/shard_map/dot_general | solution.py:61
  234.1 4.3 %fusion.2 = bf16[64,16384]{1,0:T(8,128)(2,1)S(1)} fusion(f32[16384,64]{0,1:T(8,128)S(1)} %fusion.19, f32[64,16384]{1,0:T(8,128)S(1)} %copy-done.4, f32[2,2,64,64]{3,2,1,0:T(8,128)S(1)} %copy-done.6), kind=kOutput, calls=%fused_computation.4 | convolution fusion | flops 807403520 | bytes 10518528 | tf_op jit(solution)/shard_map/dot_general | solution.py:68
  238.4 5.3 %fusion.3 = bf16[64,16384]{1,0:T(8,128)(2,1)} fusion(f32[16384,64]{0,1:T(8,128)S(1)} %fusion.21, f32[64,16384]{1,0:T(8,128)S(1)} %copy-done.5, f32[2,2,64,64]{3,2,1,0:T(8,128)S(1)} %copy-done.6), kind=kOutput, calls=%fused_computation.5 | convolution fusion | flops 807403520 | bytes 10518528 | tf_op jit(solution)/shard_map/dot_general | solution.py:63
  243.7 4.2 %stack.21 = bf16[1,2048,512]{2,1,0:T(8,128)(2,1)} reshape(bf16[64,16384]{1,0:T(8,128)(2,1)} %fusion.3) | data formatting | bytes 4194304 | tf_op jit(solution)/shard_map/stack | solution.py:71
  248.0 2.3 stack.22
  250.3 4.8 %pad_maximum_fusion.tau = bf16[2,2048,512]{2,1,0:T(8,128)(2,1)} fusion(bf16[1,2048,512]{2,1,0:T(8,128)(2,1)} %stack.22, bf16[1,2048,512]{2,1,0:T(8,128)(2,1)} %stack.21), kind=kLoop, calls=%fused_computation.17 | loop fusion | flops 2097152 | bytes 8388608 | tf_op jit(solution)/shard_map/stack | solution.py:71
  255.1 113.9 %second_sums.1 = f32[2,256,1024]{2,1,0:T(8,128)S(1)} custom-call(bf16[2,2048,512]{2,1,0:T(8,128)(2,1)} %pad_maximum_fusion.tau, bf16[2,1024,512]{2,1,0:T(8,128)(2,1)} %hist.3), custom_call_target="tpu_custom_call" | custom-call | tf_op jit(solution)/shard_map/second_sums/pallas_call | solution.py:388
  369.0 3.4 copy.8
  372.4 1.3 copy.9
  (35 shorter events, 4.9 us)
Async XLA Ops:
  7.2 0.7 copy-start
  7.2 5.1 %copy-start.2 = (bf16[2,1024,512]{2,1,0:T(8,128)(2,1)S(1)}, bf16[2,1024,512]{2,1,0:T(8,128)(2,1)}, u32[]{:S(2)}) copy-start(bf16[2,1024,512]{2,1,0:T(8,128)(2,1)} %hist.3) | copy-start | bytes 6291460
  7.2 185.2 %all-gather.2.cloned.1.call-start = ((), (), s32[]{:S(2)}) async-start(), calls=%async_computation | async-start | bytes 10485760 | tf_op jit(solution)/shard_map/all_gather | solution.py:432
  83.3 0.9 copy-start.6
  192.4 7.4 %copy-start.3 = (f32[2,2048,512]{2,1,0:T(8,128)S(1)}, f32[2,2048,512]{2,1,0:T(8,128)}, u32[]{:S(2)}) copy-start(f32[2,2048,512]{2,1,0:T(8,128)} %all-gather.2.cloned.1.call-done) | copy-start | bytes 25165828
  224.1 5.8 %copy-start.4 = (f32[64,16384]{1,0:T(8,128)S(1)}, f32[64,16384]{1,0:T(8,128)}, u32[]{:S(2)}) copy-start(f32[64,16384]{1,0:T(8,128)} %squeeze.20) | copy-start | bytes 12582916
  234.1 4.4 %copy-start.5 = (f32[64,16384]{1,0:T(8,128)S(1)}, f32[64,16384]{1,0:T(8,128)}, u32[]{:S(2)}) copy-start(f32[64,16384]{1,0:T(8,128)} %squeeze.22) | copy-start | bytes 12582916
  250.3 118.6 %slice-start = ((s8[8388608]{0:T(1024)(128)(4,1)}), s8[4194304]{0:T(1024)(128)(4,1)S(1)}, s32[]{:S(2)}) async-start(s8[8388608]{0:T(1024)(128)(4,1)} %bitcast.56), calls=%async_computation.1 | async-start | bytes 8388608
  255.1 113.9 %slice-start.1 = ((s8[8388608]{0:T(1024)(128)(4,1)}), s8[4194304]{0:T(1024)(128)(4,1)S(1)}, s32[]{:S(2)}) async-start(s8[8388608]{0:T(1024)(128)(4,1)} %bitcast.56), calls=%async_computation.2 | async-start | bytes 8388608
  369.0 4.7 %copy-start.1 = (f32[32]{0:T(128)S(1)}, f32[32]{0:T(128)}, u32[]{:S(2)}) copy-start(f32[32]{0:T(128)} %param.6) | copy-start | bytes 388
Sparse Core Ops, SparseCore 0:
  90.5 101.8 all-gather.1

commit v2 on v1

--- a/solution.py
+++ b/solution.py
@@ -52,23 +52,6 @@
     return jnp.dot(
         one_hot, coupling, precision=lax.Precision.HIGHEST, preferred_element_type=jnp.float32
     )
-
-
-def dyson_apply(inverse, source):
-    group_len = inverse.shape[1]
-    flat_width = source.shape[1] * source.shape[2] // group_len
-    flat = source.reshape(2, group_len, flat_width)
-    real_out = jnp.dot(
-        inverse[0], flat[0], precision=lax.Precision.HIGHEST, preferred_element_type=jnp.float32
-    ) - jnp.dot(
-        inverse[1], flat[1], precision=lax.Precision.HIGHEST, preferred_element_type=jnp.float32
-    )
-    imag_out = jnp.dot(
-        inverse[0], flat[1], precision=lax.Precision.HIGHEST, preferred_element_type=jnp.float32
-    ) + jnp.dot(
-        inverse[1], flat[0], precision=lax.Precision.HIGHEST, preferred_element_type=jnp.float32
-    )
-    return jnp.stack([real_out, imag_out]).reshape(source.shape)
 
 
 MESH = pl.DeviceIdType.MESH
@@ -252,16 +235,70 @@
     lax.fori_loop(0, lines - 1, drain, 0)
 
 
-def second_kernel(lines, tau, hist, out, give, take, stage, land, pair_s, pair_r, hop_s, hop_r):
+def second_kernel(
+    lines, rows, tau, near, hist, out, wide, taus, give, take, stage, land,
+    local, pair_s, pair_r, hop_s, hop_r, tau_s, tau_r, wide_s, wide_r,
+):
     row = lax.axis_index("row")
     col = lax.axis_index("col")
     q, core = lax.div(col, 2), lax.rem(col, 2)
+    half = lax.div(2 * q, lines)
     strip = out.shape[1]
-    entry_barrier(row, q, core, lines, 1)
+    entry_barrier(row, q, core, lines, rows)
+
+    def span(j):
+        return pl.ds(pl.multiple_of(j * strip, strip), strip)
+
+    def spread(j, k):
+        return remote(
+            tau.at[:, span(j)],
+            taus.at[row, :, span(j)],
+            tau_s.at[j, k - 1],
+            tau_r.at[j, k - 1],
+            lax.rem(row + k, rows),
+            col,
+        )
+
+    def widen(k):
+        return remote(
+            near, wide.at[row], wide_s.at[k - 1], wide_r.at[k - 1], lax.rem(row + k, rows), col
+        )
+
+    def order(i):
+        t, way = lax.div(i, 2), lax.rem(i + half, 2)
+        d = (lines - 1 - t) * (1 - way) + t * way
+        return d, way, (d - q) * (1 - 2 * way)
+
+    def issue(d):
+        for j in (2 * d + 1 - core, 2 * d + core):
+            for k in range(1, rows):
+                spread(j, k).start()
+
+    def early(i, c):
+        d, way, far = order(i)
+
+        @pl.when(far > 0)
+        def _():
+            issue(d)
+
+        return c
+
+    lax.fori_loop(0, 2 * (lines - 1), early, 0)
+    issue(q)
+    for k in range(1, rows):
+        widen(k).start()
+    own_wide = pltpu.make_async_copy(near, wide.at[row], local.at[0])
+    own_wide.start()
+    own_tau = pltpu.make_async_copy(tau, taus.at[row], local.at[1])
+    own_tau.start()
+    own_tau.wait()
 
     def product(j):
-        at = pl.ds(pl.multiple_of(j * strip, strip), strip)
-        real_in, imag_in = tau[0, at, :], tau[1, at, :]
+        for k in range(1, rows):
+            spread(j, k).wait_recv()
+        at = span(j)
+        real_in = jnp.concatenate([taus[r, 0, at, :] for r in range(rows)], axis=1)
+        imag_in = jnp.concatenate([taus[r, 1, at, :] for r in range(rows)], axis=1)
         real = -mm(real_in, hist[0], NT) - mm(imag_in, hist[1], NT)
         imag = mm(real_in, hist[1], NT) - mm(imag_in, hist[0], NT)
         return real, imag
@@ -297,9 +334,7 @@
             out[p] += land[way, d, p].astype(jnp.float32)
 
     def step(i, c):
-        t, way = lax.div(i, 2), lax.rem(i, 2)
-        d = (lines - 1 - t) * (1 - way) + t * way
-        far = (d - q) * (1 - 2 * way)
+        d, way, far = order(i)
 
         @pl.when(far > 0)
         def _():
@@ -346,6 +381,16 @@
         return c
 
     lax.fori_loop(0, lines, drain, 0)
+
+    def drain_tau(j, c):
+        for k in range(1, rows):
+            spread(j, k).wait_send()
+        return c
+
+    lax.fori_loop(0, 2 * lines, drain_tau, 0)
+    for k in range(1, rows):
+        widen(k).wait()
+    own_wide.wait()
 
 
 VMEM = pl.BlockSpec(memory_space=pltpu.VMEM)
@@ -381,30 +426,55 @@
     )(sigma, history)
 
 
-def second_sums(tau, history, lines):
+def second_sums(tau, near, history, lines, rows):
     depth = history.shape[1]
     strip = tau.shape[1] // (2 * lines)
     bf16 = jnp.bfloat16
     return pl.pallas_call(
-        functools.partial(second_kernel, lines),
-        out_shape=jax.ShapeDtypeStruct((2, strip, depth), jnp.float32),
-        in_specs=[VMEM] * 2,
-        out_specs=VMEM,
+        functools.partial(second_kernel, lines, rows),
+        out_shape=(
+            jax.ShapeDtypeStruct((2, strip, depth), jnp.float32),
+            jax.ShapeDtypeStruct((rows,) + near.shape, bf16),
+        ),
+        in_specs=[VMEM] * 3,
+        out_specs=(VMEM, pl.BlockSpec(memory_space=pl.ANY)),
         scratch_shapes=[
+            pltpu.VMEM((rows,) + tau.shape, bf16),
             pltpu.VMEM((lines, 2, strip, depth), bf16),
             pltpu.VMEM((lines, 2, strip, depth), bf16),
             pltpu.VMEM((lines, 2, strip, depth), bf16),
             pltpu.VMEM((2, lines, 2, strip, depth), bf16),
+            DMA((2,)),
             DMA((lines,)),
             DMA((lines,)),
             DMA((lines,)),
             DMA((2, lines)),
+            DMA((2 * lines, rows - 1)),
+            DMA((2 * lines, rows - 1)),
+            DMA((rows - 1,)),
+            DMA((rows - 1,)),
         ],
         compiler_params=pltpu.CompilerParams(
-            collective_id=1, has_side_effects=True, vmem_limit_bytes=50 * 1024 * 1024
+            collective_id=1, has_side_effects=True, vmem_limit_bytes=52 * 1024 * 1024
         ),
         name="second_sums",
-    )(tau, history)
+    )(tau, near, history)
+
+
+def stacked_dyson(inverse, source):
+    group_len = inverse.shape[1]
+    matrix = jnp.concatenate(
+        [
+            jnp.concatenate([inverse[0], -inverse[1]], axis=1),
+            jnp.concatenate([inverse[1], inverse[0]], axis=1),
+        ],
+        axis=0,
+    )
+    flat = source.reshape(2 * group_len, -1)
+    solved = jnp.dot(
+        matrix, flat, precision=lax.Precision.HIGHEST, preferred_element_type=jnp.float32
+    )
+    return solved.reshape(source.shape)
 
 
 def shards(history, start_strip, coupling, dyson_inverse):
@@ -416,29 +486,39 @@
     strip_cols = start_strip.shape[2]
     group_rows = strip_rows * col_count
     tile_cols = history.shape[2]
+    share_cols = tile_cols // row_count
     sigma_first = self_energy(
         start_strip,
         orbital_weights(coupling, col_index * strip_rows, strip_rows),
         orbital_weights(coupling, row_index * strip_cols, strip_cols),
     ).astype(jnp.bfloat16)
-    if tile_cols // row_count % 128 == 0:
+    fits = share_cols % 128 == 0
+    if fits:
         shares = first_sums(sigma_first, history, col_count // 2, row_count)
     else:
         partial_first = complex_product(
             lax.all_gather(sigma_first, "col", axis=1, tiled=True), history
         )
         shares = lax.psum_scatter(partial_first, "row", scatter_dimension=2, tiled=True)
-    solved_part = dyson_apply(dyson_inverse[0], TIME_STEP * shares)
-    earlier = lax.all_gather(solved_part, "row", axis=2, tiled=True)
+    solved_part = stacked_dyson(dyson_inverse[0], TIME_STEP * shares)
     sigma_second = self_energy(
-        earlier,
+        solved_part,
         orbital_weights(coupling, 0, group_rows),
-        orbital_weights(coupling, col_index * tile_cols, tile_cols),
+        orbital_weights(coupling, col_index * tile_cols + row_index * share_cols, share_cols),
     ).astype(jnp.bfloat16)
-    solved_sigma = dyson_apply(
+    solved_sigma = stacked_dyson(
         dyson_inverse[1], TIME_STEP * sigma_second.astype(jnp.float32)
     ).astype(jnp.bfloat16)
-    later_strip = second_sums(solved_sigma, history, col_count // 2)
+    if fits:
+        later_strip, wide = second_sums(
+            solved_sigma, solved_part.astype(jnp.bfloat16), history, col_count // 2, row_count
+        )
+        earlier = jnp.transpose(wide, (1, 2, 0, 3)).reshape(2, group_rows, tile_cols)
+        return (earlier.astype(jnp.float32), later_strip)
+    earlier = lax.all_gather(solved_part, "row", axis=2, tiled=True)
+    tau = lax.all_gather(solved_sigma, "row", axis=2, tiled=True)
+    partial_second = mirror_product(tau, history)
+    later_strip = lax.psum_scatter(partial_second, "col", scatter_dimension=1, tiled=True)
     return (earlier, later_strip)
 
 

time: 382 us -> 238 us (0.62)
  waiting for transfers between devices: 101 us -> 0 us
  matrix products: 25.6 us -> 8.67 us
  between operations: 14.3 us -> 0.77 us
  other arithmetic: 22.4 us -> 11.1 us
    all_gather x1 -> x0, waiting for transfers between devices: 101 us -> none  [shards(): earlier = lax.all_gather(solved_part, 'row', axis=2, tiled=True)]
    dot_general x8 -> x2, matrix products: 23.9 us -> 7.11 us  [stacked_dyson(): jnp.dot(matrix, flat, precision=lax.Precision.HIGHEST, preferred_element_...]
    convert_element_type x0 -> x3, local copies, waits for them, and re-layouts: none -> 10.6 us  [the longest x1 8.75 us: shards(): return (earlier.astype(jnp.float32), later_strip)]
    squeeze x4 -> x1, local copies, waits for them, and re-layouts: 10.3 us -> 0.82 us  [stacked_dyson(): inverse[1]]
    slice x2 -> x0, local copies, waits for them, and re-layouts: 7.82 us -> none  [dyson_apply(): flat[0]]
    another operation x4 -> x0, local copies, waits for them, and re-layouts: 6.89 us -> none  [dyson_apply(): return jnp.stack([real_out, imag_out]).reshape(source.shape)]
    another operation x2 -> x0, other arithmetic: 6.22 us -> none  [dyson_apply(): return jnp.stack([real_out, imag_out]).reshape(source.shape)]
    convert_element_type x0 -> x1, other arithmetic: none -> 6.13 us  [shards(): return (earlier.astype(jnp.float32), later_strip)]
  transfers between devices with their start and end apart: 1 -> 0, of which waited for: 1 -> 0; matrix products, arithmetic and copies ran while one was open for 0% -> 0% of each run, Pallas kernels for 0% -> 0%
where the time goes in v2:
time: 238 us; the launch traced here: 236 us
  Pallas kernels  185 us (78%)
  local copies, waits for them, and re-layouts  30.2 us (13%)
  other arithmetic  11.1 us (5%)
  matrix products  8.67 us (4%)
    pallas_call x1, Pallas kernels, second_sums(): pl.pallas_call(functools.partial(second_kernel, lines, rows), out_shape=(...  114 us
    pallas_call x1, Pallas kernels, first_sums(): pl.pallas_call(functools.partial(first_kernel, lines, rows), out_shape=ja...  70.8 us
    unnamed x10, local copies, waits for them, and re-layouts  12 us
    convert_element_type x1, local copies, waits for them, and re-layouts, shards(): return (earlier.astype(jnp.float32), later_strip)  8.75 us
    dot_general x2, matrix products, stacked_dyson(): jnp.dot(matrix, flat, precision=lax.Precision.HIGHEST, preferred_element_...  7.11 us
    convert_element_type x1, other arithmetic, shards(): return (earlier.astype(jnp.float32), later_strip)  6.13 us

profile of v2, /device:TPU:9, one launch (start us, length us, event | category | flops | bytes accessed | tf_op | source)
XLA Modules:
  0.0 235.6 jit_solution(15487108477424177135)
XLA Ops:
  0.7 0.6 copy-done
  1.6 0.2 fusion.8
  1.8 0.4 fusion.6
  2.3 0.7 fusion.4
  3.0 0.8 fusion.42
  3.8 0.8 slice_bitcast_fusion.2
  4.6 1.8 multiply_bitcast_fusion
  6.4 0.4 multiply_convert_fusion.1.sig
  6.8 1.2 copy-done.1
  8.0 70.8 %first_sums.1 = f32[2,2048,128]{2,1,0:T(8,128)S(1)} custom-call(bf16[2,256,1024]{2,1,0:T(8,128)(2,1)S(1)} %multiply_convert_fusion.1.sig, bf16[2,1024,512]{2,1,0:T(8,128)(2,1)S(1)} %copy-done.1), custom_call_target="tpu_custom_call" | custom-call | tf_op jit(solution)/shard_map/first_sums/pallas_call | solution.py:405
  79.0 1.5 reshape.171
  80.5 3.5 %fusion.44 = (bf16[128,4096]{1,0:T(8,128)(2,1)S(1)}, f32[128,4096]{1,0:T(8,128)S(1)}) fusion(f32[128,4096]{1,0:T(8,128)} %reshape.171, f32[64,64]{1,0:T(8,128)S(1)} %get-tuple-element.13, f32[64,64]{1,0:T(8,128)S(1)} %get-tuple-element.12, f32[64,64]{1,0:T(8,128)S(1)} %get-tuple-element.9), kind=kOutput, calls=%fused_computation.73 | convolution fusion | flops 805879808 | bytes 5292032 | tf_op jit(solution)/shard_map/dot_general | solution.py:474
  84.0 1.3 convert_element_type.40.near
  85.5 1.1 add.100
  86.6 1.6 negate_multiply_fusion
  88.2 1.5 mul.132
  89.6 2.7 %mul.133 = f32[128,4096]{1,0:T(8,128)} reshape(f32[2,2048,128]{2,1,0:T(8,128)} %mul.132) | data formatting | bytes 4194304 | tf_op jit(solution)/shard_map/mul | solution.py:43
  92.3 3.6 %convolution_convert_fusion = bf16[128,4096]{1,0:T(8,128)(2,1)S(1)} fusion(f32[128,4096]{1,0:T(8,128)S(1)} %get-tuple-element.15, f32[128,4096]{1,0:T(8,128)} %mul.133, f32[64,64]{1,0:T(8,128)S(1)} %get-tuple-element.11, f32[64,64]{1,0:T(8,128)S(1)} %get-tuple-element.10, f32[64,64]{1,0:T(8,128)S(1)} %get-tuple-element.8), kind=kOutput, calls=%fused_computation.1 | convolution fusion | flops 807976960 | bytes 5292032 | tf_op jit(solution)/shard_map/dot_general | solution.py:474
  96.0 0.5 convert_element_type.38.tau
  96.5 114.1 %second_sums.1 = (f32[2,256,1024]{2,1,0:T(8,128)}, bf16[4,2,2048,128]{3,2,1,0:T(8,128)(2,1)}) custom-call(bf16[2,2048,128]{2,1,0:T(8,128)(2,1)S(1)} %convert_element_type.38.tau, bf16[2,2048,128]{2,1,0:T(8,128)(2,1)} %convert_element_type.40.near, bf16[2,1024,512]{2,1,0:T(8,128)(2,1)} %hist.3), custom_call_target="tpu_custom_call" | custom-call | tf_op jit(solution)/shard_map/second_sums/pallas_call | solution.py:433
  210.6 6.1 %convert_bitcast_fusion = f32[2,2048,4,128]{3,1,0,2:T(8,128)} fusion(bf16[4,2,2048,128]{3,2,1,0:T(8,128)(2,1)} %get-tuple-element.4), kind=kLoop, calls=%fused_computation | loop fusion | flops 2097152 | bytes 12582912 | tf_op jit(solution)/shard_map/convert_element_type | solution.py:517
  216.7 8.7 %copy.6 = f32[2,2048,4,128]{1,3,2,0:T(8,128)} copy(f32[2,2048,4,128]{3,1,0,2:T(8,128)} %convert_bitcast_fusion) | data formatting | bytes 16777216 | tf_op jit(solution)/shard_map/convert_element_type | solution.py:517
  225.5 8.8 %copy.7 = f32[2,2048,512]{2,1,0:T(8,128)} copy(f32[2,2048,512]{1,2,0:T(8,128)} %bitcast.35) | data formatting | bytes 16777216
  234.3 1.3 copy.9
  (13 shorter events, 0.7 us)
Async XLA Ops:
  0.6 0.7 copy-start
  0.6 5.8 %copy-start.2 = (f32[2,256,1024]{2,1,0:T(8,128)S(1)}, f32[2,256,1024]{2,1,0:T(8,128)}, u32[]{:S(2)}) copy-start(f32[2,256,1024]{2,1,0:T(8,128)} %param.5) | copy-start | bytes 6291460
  6.4 1.6 copy-start.1
  225.5 8.8 %copy-start.3 = (f32[2,256,1024]{2,1,0:T(8,128)S(1)}, f32[2,256,1024]{2,1,0:T(8,128)}, u32[]{:S(2)}) copy-start(f32[2,256,1024]{2,1,0:T(8,128)} %get-tuple-element.19) | copy-start | bytes 6291460

commit v3 on v2

--- a/solution.py
+++ b/solution.py
@@ -259,10 +259,23 @@
             col,
         )
 
+    share = near.shape[2]
+    mesh_2x2 = rows == 4
+    beside = row + 1 - 2 * lax.rem(row, 2)
+    across = lax.rem(row + 2, 4)
+    direct = [beside, across] if mesh_2x2 else [lax.rem(row + k, rows) for k in range(1, rows)]
+
+    def columns(r):
+        return pl.ds(pl.multiple_of(r * share, share), share)
+
+    mine = wide.at[:, :, columns(row)]
+
     def widen(k):
-        return remote(
-            near, wide.at[row], wide_s.at[k - 1], wide_r.at[k - 1], lax.rem(row + k, rows), col
-        )
+        return remote(near, mine, wide_s.at[k], wide_r.at[k], direct[k], col)
+
+    def relay(k):
+        block = wide.at[k, :, columns(direct[k])]
+        return remote(block, block, wide_s.at[2 + k], wide_r.at[2 + k], direct[1 - k], col)
 
     def order(i):
         t, way = lax.div(i, 2), lax.rem(i + half, 2)
@@ -285,9 +298,9 @@
 
     lax.fori_loop(0, 2 * (lines - 1), early, 0)
     issue(q)
-    for k in range(1, rows):
+    for k in range(len(direct)):
         widen(k).start()
-    own_wide = pltpu.make_async_copy(near, wide.at[row], local.at[0])
+    own_wide = pltpu.make_async_copy(near, mine, local.at[0])
     own_wide.start()
     own_tau = pltpu.make_async_copy(tau, taus.at[row], local.at[1])
     own_tau.start()
@@ -356,6 +369,11 @@
         return c
 
     lax.fori_loop(0, 2 * (lines - 1), step, 0)
+    if mesh_2x2:
+        for k in (0, 1):
+            widen(k).wait_recv()
+        for k in (0, 1):
+            relay(k).start()
     offer(q)
     gather(q)
 
@@ -388,8 +406,12 @@
         return c
 
     lax.fori_loop(0, 2 * lines, drain_tau, 0)
-    for k in range(1, rows):
-        widen(k).wait()
+    for k in range(len(direct)):
+        widen(k).wait_send()
+        if mesh_2x2:
+            relay(k).wait()
+        else:
+            widen(k).wait_recv()
     own_wide.wait()
 
 
@@ -434,7 +456,7 @@
         functools.partial(second_kernel, lines, rows),
         out_shape=(
             jax.ShapeDtypeStruct((2, strip, depth), jnp.float32),
-            jax.ShapeDtypeStruct((rows,) + near.shape, bf16),
+            jax.ShapeDtypeStruct(near.shape[:2] + (rows * near.shape[2],), bf16),
         ),
         in_specs=[VMEM] * 3,
         out_specs=(VMEM, pl.BlockSpec(memory_space=pl.ANY)),
@@ -451,8 +473,8 @@
             DMA((2, lines)),
             DMA((2 * lines, rows - 1)),
             DMA((2 * lines, rows - 1)),
-            DMA((rows - 1,)),
-            DMA((rows - 1,)),
+            DMA((max(rows - 1, 4),)),
+            DMA((max(rows - 1, 4),)),
         ],
         compiler_params=pltpu.CompilerParams(
             collective_id=1, has_side_effects=True, vmem_limit_bytes=52 * 1024 * 1024
@@ -463,7 +485,7 @@
 
 def stacked_dyson(inverse, source):
     group_len = inverse.shape[1]
-    matrix = jnp.concatenate(
+    matrix = TIME_STEP * jnp.concatenate(
         [
             jnp.concatenate([inverse[0], -inverse[1]], axis=1),
             jnp.concatenate([inverse[1], inverse[0]], axis=1),
@@ -500,21 +522,20 @@
             lax.all_gather(sigma_first, "col", axis=1, tiled=True), history
         )
         shares = lax.psum_scatter(partial_first, "row", scatter_dimension=2, tiled=True)
-    solved_part = stacked_dyson(dyson_inverse[0], TIME_STEP * shares)
+    solved_part = stacked_dyson(dyson_inverse[0], shares)
     sigma_second = self_energy(
         solved_part,
         orbital_weights(coupling, 0, group_rows),
         orbital_weights(coupling, col_index * tile_cols + row_index * share_cols, share_cols),
     ).astype(jnp.bfloat16)
     solved_sigma = stacked_dyson(
-        dyson_inverse[1], TIME_STEP * sigma_second.astype(jnp.float32)
+        dyson_inverse[1], sigma_second.astype(jnp.float32)
     ).astype(jnp.bfloat16)
     if fits:
         later_strip, wide = second_sums(
             solved_sigma, solved_part.astype(jnp.bfloat16), history, col_count // 2, row_count
         )
-        earlier = jnp.transpose(wide, (1, 2, 0, 3)).reshape(2, group_rows, tile_cols)
-        return (earlier.astype(jnp.float32), later_strip)
+        return (wide.astype(jnp.float32), later_strip)
     earlier = lax.all_gather(solved_part, "row", axis=2, tiled=True)
     tau = lax.all_gather(solved_sigma, "row", axis=2, tiled=True)
     partial_second = mirror_product(tau, history)

time: 238 us -> 218 us (0.916)
  local copies, waits for them, and re-layouts: 30.2 us -> 12.7 us
    unnamed x10 -> x9, local copies, waits for them, and re-layouts: 12 us -> 3.16 us
    convert_element_type x2 -> x1, local copies, waits for them, and re-layouts: 9.28 us -> 0.53 us  [shards(): solved_sigma = stacked_dyson(dyson_inverse[1], sigma_second.astype(jnp.fl...]
where the time goes in v3:
time: 218 us
  Pallas kernels  185 us (85%)
  local copies, waits for them, and re-layouts  12.7 us (6%)
  other arithmetic  11.7 us (5%)
  matrix products  7.78 us (4%)
    pallas_call x1, Pallas kernels, second_sums(): pl.pallas_call(functools.partial(second_kernel, lines, rows), out_shape=(...  114 us
    pallas_call x1, Pallas kernels, first_sums(): pl.pallas_call(functools.partial(first_kernel, lines, rows), out_shape=ja...  70.8 us
    convert_element_type x1, other arithmetic, shards(): return (wide.astype(jnp.float32), later_strip)  6.93 us
    dot_general x2, matrix products, stacked_dyson(): jnp.dot(matrix, flat, precision=lax.Precision.HIGHEST, preferred_element_...  6.22 us

profile of v3, /device:TPU:9, one launch (start us, length us, event | category | flops | bytes accessed | tf_op | source)
XLA Modules:
  0.0 217.8 jit_solution(4454967567926858095)
XLA Ops:
  0.7 0.6 copy-done
  1.3 0.2 convolution_bitcast_fusion
  1.6 0.2 fusion.5
  1.8 0.4 fusion.3
  2.3 0.7 fusion.1
  3.0 0.8 fusion.40
  3.8 0.8 slice_bitcast_fusion.2
  4.6 1.8 multiply_bitcast_fusion
  6.4 0.4 multiply_convert_fusion.1.sig
  6.8 1.2 copy-done.1
  8.0 70.8 %first_sums.1 = f32[2,2048,128]{2,1,0:T(8,128)S(1)} custom-call(bf16[2,256,1024]{2,1,0:T(8,128)(2,1)S(1)} %multiply_convert_fusion.1.sig, bf16[2,1024,512]{2,1,0:T(8,128)(2,1)S(1)} %copy-done.1), custom_call_target="tpu_custom_call" | custom-call | tf_op jit(solution)/shard_map/first_sums/pallas_call | solution.py:427
  78.8 1.5 reshape.168
  80.3 3.5 %fusion.42 = (bf16[128,4096]{1,0:T(8,128)(2,1)S(1)}, f32[128,4096]{1,0:T(8,128)S(1)}) fusion(f32[128,4096]{1,0:T(8,128)} %reshape.168, f32[64,64]{1,0:T(8,128)S(1)} %get-tuple-element.11, f32[64,64]{1,0:T(8,128)S(1)} %get-tuple-element.10, f32[64,64]{1,0:T(8,128)S(1)} %get-tuple-element.7), kind=kOutput, calls=%fused_computation.71 | convolution fusion | flops 805896192 | bytes 5292032 | tf_op jit(solution)/shard_map/dot_general | solution.py:496
  83.8 1.3 convert_element_type.30.near
  85.1 0.1 fusion
  85.3 1.1 add.100
  86.4 1.6 negate_multiply_fusion
  88.0 1.5 mul.132
  89.4 2.7 %mul.133 = f32[128,4096]{1,0:T(8,128)} reshape(f32[2,2048,128]{2,1,0:T(8,128)} %mul.132) | data formatting | bytes 4194304 | tf_op jit(solution)/shard_map/mul | solution.py:43
  92.1 2.7 %convolution_convert_fusion = bf16[128,4096]{1,0:T(8,128)(2,1)S(1)} fusion(f32[128,4096]{1,0:T(8,128)S(1)} %get-tuple-element.13, f32[128,4096]{1,0:T(8,128)} %mul.133, f32[64,64]{1,0:T(8,128)S(1)} %get-tuple-element.9, f32[64,64]{1,0:T(8,128)S(1)} %get-tuple-element.8, f32[64,64]{1,0:T(8,128)S(1)} %get-tuple-element.6), kind=kOutput, calls=%fused_computation | convolution fusion | flops 806944768 | bytes 5292032 | tf_op jit(solution)/shard_map/dot_general | solution.py:496
  94.9 0.5 convert_element_type.28.tau
  95.4 114.1 %second_sums.1 = (f32[2,256,1024]{2,1,0:T(8,128)}, bf16[2,2048,512]{2,1,0:T(8,128)(2,1)}) custom-call(bf16[2,2048,128]{2,1,0:T(8,128)(2,1)S(1)} %convert_element_type.28.tau, bf16[2,2048,128]{2,1,0:T(8,128)(2,1)} %convert_element_type.30.near, bf16[2,1024,512]{2,1,0:T(8,128)(2,1)} %hist.3), custom_call_target="tpu_custom_call" | custom-call | tf_op jit(solution)/shard_map/second_sums/pallas_call | solution.py:455
  209.5 6.9 %convert_element_type.31 = f32[2,2048,512]{2,1,0:T(8,128)} convert(bf16[2,2048,512]{2,1,0:T(8,128)(2,1)} %get-tuple-element.4) | non-fusion elementwise | flops 2097152 | bytes 12582912 | tf_op jit(solution)/shard_map/convert_element_type | solution.py:538
  216.4 1.3 copy.7
  (10 shorter events, 0.2 us)
Async XLA Ops:
  0.6 0.7 copy-start
  0.6 5.8 %copy-start.2 = (f32[2,256,1024]{2,1,0:T(8,128)S(1)}, f32[2,256,1024]{2,1,0:T(8,128)}, u32[]{:S(2)}) copy-start(f32[2,256,1024]{2,1,0:T(8,128)} %param.5) | copy-start | bytes 6291460
  6.4 1.6 copy-start.1
  209.5 6.9 %copy-start.3 = (f32[2,256,1024]{2,1,0:T(8,128)S(1)}, f32[2,256,1024]{2,1,0:T(8,128)}, u32[]{:S(2)}) copy-start(f32[2,256,1024]{2,1,0:T(8,128)} %get-tuple-element.17) | copy-start | bytes 6291460
